TPU v7x, 256 devices: a whole 4x4x8 slice. The times are simulated.
256 devices in a mesh: row: 16 (over x, y), col: 16 (over z, core).
Axes of the slice: x: 4, y: 4, z: 8, core: 2. Of those that a mesh axis runs over, the one named last changes fastest.
Arguments:
- target: float32 [8, 16, 128, 8, 16, 128], P(None, 'row', None, None, 'col'), may hold values from -6 to 6
- panel_a: bfloat16 [2, 32, 128, 512], P(None, 'col'), may hold values from -1.1953125 to 1.1953125
- inv_factor: bfloat16 [2, 512, 512], replicated, as said below
- panel_rhs: bfloat16 [2, 512, 256], P(None, 'col'), may hold values from -6 to 6
- panel_rows: int32 [2, 32], replicated, may hold values from 0 to 127, as said below
- right_sides: float32 [8, 16, 128, 256], P(None, 'col'), may hold values from -12 to 12
Outputs:
- updated_target: float32 [8, 16, 128, 8, 16, 128], P(None, 'row', None, None, 'col')
- updated_sides: float32 [8, 16, 128, 256], P(None, 'col')
Inputs may be any that keep to these rules, and one draw needn't show every extreme that they name: `panel_rows`: each row holds 32 distinct positions in increasing order, the first 0 and the last 127. `inv_factor`: lower triangular, diagonal between 0.5 and 2.
All inputs are finite; a program needn't handle non-finite values.
Results may differ from a plain program's by a relative error of at most 0.0035.
Values may be sent and summed in bfloat16 or wider, within the bound.
A program may use at most 128 MiB of HBM per device.

v0:
```python
import jax
import jax.numpy as jnp
from jax import lax
from jax.sharding import PartitionSpec as P


def shards(target, panel_a, inv_factor, panel_rhs, panel_rows, right_sides):
    row_count = lax.axis_size("row")
    col_count = lax.axis_size("col")
    row_index = lax.axis_index("row")
    col_index = lax.axis_index("col")
    tile_rows = target.shape[2]
    row_blocks = target.shape[0]
    col_blocks = target.shape[3]
    slab_rows = tile_rows // row_count
    shard_rows = panel_rhs.shape[1]
    updated_target = target
    updated_sides = right_sides
    row_places = jnp.arange(row_blocks, dtype=jnp.int32) * row_count + row_index
    col_places = jnp.arange(col_blocks, dtype=jnp.int32) * col_count + col_index
    for which_panel in range(2):
        factor = inv_factor[which_panel]
        positions = panel_rows[which_panel]
        own_rows = lax.dynamic_slice_in_dim(
            panel_a[which_panel], row_index * slab_rows, slab_rows, 1
        )
        solved_piece = jnp.einsum(
            "axq,pq->axp", own_rows, factor, preferred_element_type=jnp.float32
        ).astype(jnp.bfloat16)
        column_tiles = lax.all_gather(solved_piece, "row", axis=1, tiled=True)
        all_tiles = lax.all_gather(column_tiles, "col", axis=0, tiled=True)
        columns = lax.dynamic_slice_in_dim(factor, col_index * shard_rows, shard_rows, 1)
        local_term = jnp.dot(columns, panel_rhs[which_panel], preferred_element_type=jnp.float32)
        partial_value = lax.psum(local_term, "col").astype(jnp.bfloat16)
        pick_rows = (positions[None, :] == row_places[:, None]).astype(jnp.bfloat16)
        pick_cols = (positions[None, :] == col_places[:, None]).astype(jnp.bfloat16)
        row_set = jnp.einsum(
            "ia,axp->ixp", pick_rows, all_tiles, preferred_element_type=jnp.float32
        ).astype(jnp.bfloat16)
        col_set = jnp.einsum(
            "ka,axp->kxp", pick_cols, all_tiles, preferred_element_type=jnp.float32
        ).astype(jnp.bfloat16)
        schur_term = jnp.einsum(
            "ixp,kyp->ixky", row_set, col_set, preferred_element_type=jnp.float32
        )
        updated_target = updated_target - schur_term[:, None, :, :, None, :]
        side_term = jnp.einsum(
            "kxp,pn->kxn", col_set, partial_value, preferred_element_type=jnp.float32
        )
        updated_sides = updated_sides - side_term[:, None]
    return (updated_target, updated_sides)


def solution(mesh):
    placed = (
        P(None, "row", None, None, "col", None),
        P(None, "col", None, None),
        P(),
        P(None, "col", None),
        P(),
        P(None, "col", None, None),
    )
    return jax.shard_map(
        shards,
        mesh=mesh,
        in_specs=placed,
        out_specs=(P(None, "row", None, None, "col", None), P(None, "col", None, None)),
        check_vma=False,
    )
```

profile of v0, /device:TPU:0, one launch (start us, length us, event | category | flops | bytes accessed | tf_op | source)
XLA Modules:
  0.0 168.0 jit_solution(11555292527745360764)
XLA Ops:
  7.2 0.0 all-gather.5.cloned.1.call-start
  7.2 1.1 fusion.73
  8.3 1.3 convolution_convert_fusion
  9.6 24.2 %all_gather.14 = bf16[2,128,512]{2,1,0:T(8,128)(2,1)} all-gather(bf16[2,8,512]{2,1,0:T(8,128)(2,1)S(1)} %convolution_convert_fusion), channel_id=1, replica_groups=mesh['row'=16,'col'=16] {'row'}, dimensions={1}, use_global_device_ids=true | all-gather | bytes 278528 | tf_op jit(solution)/shard_map/all_gather | solution.py:30
  33.8 0.0 all-gather.5.cloned.1.call-update
  33.8 0.0 all-gather.3.cloned.1.call-start
  33.9 1.3 convolution_convert_fusion.1
  35.2 25.0 %all_gather.12 = bf16[2,128,512]{2,1,0:T(8,128)(2,1)} all-gather(bf16[2,8,512]{2,1,0:T(8,128)(2,1)S(1)} %convolution_convert_fusion.1), channel_id=1, replica_groups=mesh['row'=16,'col'=16] {'row'}, dimensions={1}, use_global_device_ids=true | all-gather | bytes 278528 | tf_op jit(solution)/shard_map/all_gather | solution.py:30
  60.2 0.0 all-gather.3.cloned.1.call-update
  60.2 1.3 fusion.72
  61.5 0.3 fusion.34
  61.8 0.3 fusion.36
  62.1 69.4 %all-reduce.2 = (bf16[512,256]{1,0:T(8,128)(2,1)S(1)}, bf16[512,256]{1,0:T(8,128)(2,1)S(1)}) all-reduce(f32[512,256]{1,0:T(8,128)S(1)} %fusion.34, f32[512,256]{1,0:T(8,128)S(1)} %fusion.36), channel_id=1, replica_groups=mesh['row'=16,'col'=16] {'col'}, use_global_device_ids=true, to_apply=%region_1.0 | all-reduce | flops 262144 | bytes 1572864 | tf_op jit(solution)/shard_map/psum | solution.py:34
  131.6 0.0 all-gather.5.cloned.1.call-done
  131.6 4.5 %fusion.11 = bf16[8,128,512]{2,0,1:T(8,128)(2,1)S(1)} fusion(bf16[32,128,512]{2,1,0:T(8,128)(2,1)} %all-gather.5.cloned.1.call-done, s32[32]{0:T(128)S(1)} %get-tuple-element.12, s32[8]{0:T(128)S(1)} %fusion.68), kind=kOutput, calls=%fused_computation.13 | convolution fusion | flops 34078976 | bytes 5243040 | tf_op jit(solution)/shard_map/ka,axp->kxp/dot_general | solution.py:40
  136.2 1.7 %convolution_bitcast_fusion = f32[8,1,128,256]{3,2,0,1:T(8,128)} fusion(bf16[8,128,512]{2,0,1:T(8,128)(2,1)S(1)} %fusion.11, bf16[512,256]{1,0:T(8,128)(2,1)S(1)} %get-tuple-element.6), kind=kOutput, calls=%fused_computation.14 | convolution fusion | flops 268435456 | bytes 2359296 | tf_op jit(solution)/shard_map/kxp,pn->kxn/dot_general | solution.py:47
  137.9 4.7 %fusion.8 = bf16[8,128,512]{2,0,1:T(8,128)(2,1)S(1)} fusion(bf16[32,128,512]{2,1,0:T(8,128)(2,1)} %all-gather.3.cloned.1.call-done, s32[32]{0:T(128)S(1)} %get-tuple-element.13, s32[8]{0:T(128)S(1)} %fusion.68), kind=kOutput, calls=%fused_computation.12 | convolution fusion | flops 34078976 | bytes 5243040 | tf_op jit(solution)/shard_map/ka,axp->kxp/dot_general | solution.py:40
  142.6 2.4 %fusion.4 = bf16[8,128,512]{2,0,1:T(8,128)(2,1)S(1)} fusion(bf16[32,128,512]{2,1,0:T(8,128)(2,1)S(1)} %copy-done.1, s32[32]{0:T(128)S(1)} %get-tuple-element.13, s32[8]{0:T(128)S(1)} %fusion.69), kind=kOutput, calls=%fused_computation.6 | convolution fusion | flops 33554688 | bytes 5243040 | tf_op jit(solution)/shard_map/ia,axp->ixp/dot_general | solution.py:37
  145.0 1.6 fusion.18
  146.6 0.5 copy-done
  147.2 2.4 %fusion = bf16[8,128,512]{2,0,1:T(8,128)(2,1)S(1)} fusion(bf16[32,128,512]{2,1,0:T(8,128)(2,1)S(1)} %copy-done, s32[32]{0:T(128)S(1)} %get-tuple-element.12, s32[8]{0:T(128)S(1)} %fusion.69), kind=kOutput, calls=%fused_computation.2 | convolution fusion | flops 33554688 | bytes 5243040 | tf_op jit(solution)/shard_map/ia,axp->ixp/dot_general | solution.py:37
  149.5 2.4 %bitcast_subtract_fusion = f32[8,1,128,8,1,128]{5,2,3,0,4,1:T(8,128)S(1)} fusion(f32[8,128,8,128]{3,1,2,0:T(8,128)S(1)} %fusion.18, f32[8,1,128,8,1,128]{5,4,3,2,1,0:T(1,128)S(1)} %copy-done.2, bf16[8,128,512]{2,0,1:T(8,128)(2,1)S(1)} %fusion, bf16[8,128,512]{2,0,1:T(8,128)(2,1)S(1)} %fusion.11), kind=kOutput, calls=%fused_computation | convolution fusion | flops 1075838976 | bytes 14680064 | tf_op jit(solution)/shard_map/ixp,kyp->ixky/dot_general | solution.py:43
  151.9 6.3 %copy.26 = f32[8,1,128,8,1,128]{5,4,3,2,1,0:T(1,128)} copy(f32[8,1,128,8,1,128]{5,2,3,0,4,1:T(8,128)S(1)} %bitcast_subtract_fusion) | data formatting | bytes 8388608
  158.2 2.9 %fusion.16 = f32[8,1,128,256]{3,2,1,0:T(8,128)} fusion(f32[8,1,128,256]{3,2,0,1:T(8,128)S(1)} %copy-done.3, f32[8,1,128,256]{3,2,1,0:T(8,128)} %param.11, bf16[8,128,512]{2,0,1:T(8,128)(2,1)S(1)} %fusion.8, bf16[512,256]{1,0:T(8,128)(2,1)S(1)} %get-tuple-element.7), kind=kOutput, calls=%fused_computation.18 | convolution fusion | flops 268959744 | bytes 4456448 | tf_op jit(solution)/shard_map/kxp,pn->kxn/dot_general | solution.py:47
  (15 shorter events, 0.0 us)
Async XLA Ops:
  7.2 54.3 %copy-start.4 = (bf16[2,32,256]{2,1,0:T(8,128)(2,1)S(1)}, bf16[2,32,256]{2,1,0:T(8,128)(2,1)}, u32[]{:S(2)}) copy-start(bf16[2,32,256]{2,1,0:T(8,128)(2,1)} %param.9) | copy-start | bytes 98308
  7.2 54.9 %copy-start.5 = (s32[2,32]{1,0:T(2,128)S(1)}, s32[2,32]{1,0:T(2,128)}, u32[]{:S(2)}) copy-start(s32[2,32]{1,0:T(2,128)} %param.10) | copy-start | bytes 772
  7.2 124.4 %all-gather.5.cloned.1.call-start = ((), (), s32[]{:S(2)}) async-start(), calls=%async_computation.1 | async-start | bytes 4456448 | tf_op jit(solution)/shard_map/all_gather | solution.py:31
  33.8 104.1 %all-gather.3.cloned.1.call-start = ((), (), s32[]{:S(2)}) async-start(), calls=%async_computation | async-start | bytes 4456448 | tf_op jit(solution)/shard_map/all_gather | solution.py:31
  137.9 4.7 %copy-start.1 = (bf16[32,128,512]{2,1,0:T(8,128)(2,1)S(1)}, bf16[32,128,512]{2,1,0:T(8,128)(2,1)}, u32[]{:S(2)}) copy-start(bf16[32,128,512]{2,1,0:T(8,128)(2,1)} %all-gather.3.cloned.1.call-done) | copy-start | bytes 12582916
  145.0 2.2 %copy-start = (bf16[32,128,512]{2,1,0:T(8,128)(2,1)S(1)}, bf16[32,128,512]{2,1,0:T(8,128)(2,1)}, u32[]{:S(2)}) copy-start(bf16[32,128,512]{2,1,0:T(8,128)(2,1)} %all-gather.5.cloned.1.call-done) | copy-start | bytes 12582916
  147.2 2.4 %copy-start.2 = (f32[8,1,128,8,1,128]{5,4,3,2,1,0:T(1,128)S(1)}, f32[8,1,128,8,1,128]{5,4,3,2,1,0:T(1,128)}, u32[]{:S(2)}) copy-start(f32[8,1,128,8,1,128]{5,4,3,2,1,0:T(1,128)} %param.6) | copy-start | bytes 12582916
  151.9 6.3 %copy-start.3 = (f32[8,1,128,256]{3,2,0,1:T(8,128)S(1)}, f32[8,1,128,256]{3,2,0,1:T(8,128)}, u32[]{:S(2)}) copy-start(f32[8,1,128,256]{3,2,0,1:T(8,128)} %convolution_bitcast_fusion) | copy-start | bytes 3145732
Sparse Core Ops, SparseCore 0:
  33.9 43.4 all-gather.4
  79.3 43.1 all-gather.2
where the time goes:
time: 168 us
  blocking collectives  119 us (71%)
  matrix products  25.8 us (15%)
  between operations  14.2 us (8%)
  local copies, waits for them, and re-layouts  9.27 us (6%)
    psum x1, blocking collectives, shards(): partial_value = lax.psum(local_term, 'col').astype(jnp.bfloat16)  69.4 us
    all_gather x2, blocking collectives, shards(): column_tiles = lax.all_gather(solved_piece, 'row', axis=1, tiled=True)  49.2 us
    dot_general x2, matrix products, shards(): jnp.einsum('ka,axp->kxp', pick_cols, all_tiles, preferred_element_type=jn...  9.25 us
    unnamed x13, local copies, waits for them, and re-layouts  6.89 us
    dot_general x2, matrix products, shards(): jnp.einsum('ia,axp->ixp', pick_rows, all_tiles, preferred_element_type=jn...  4.72 us
    dot_general x2, matrix products, shards(): jnp.einsum('kxp,pn->kxn', col_set, partial_value, preferred_element_type=...  4.65 us
    dot_general x2, matrix products, shards(): jnp.einsum('ixp,kyp->ixky', row_set, col_set, preferred_element_type=jnp....  4 us
  transfers between devices with their start and end apart: 2, of which 0 were waited for; matrix products, arithmetic and copies ran while one was open for 6% of the time, Pallas kernels for 0%

commit v1 on v0

--- a/solution.py
+++ b/solution.py
@@ -2,6 +2,12 @@
 import jax.numpy as jnp
 from jax import lax
 from jax.sharding import PartitionSpec as P
+
+
+def add_all(x, axis):
+    parts = lax.all_gather(x, axis, axis=0, tiled=False)
+    total = parts.sum(axis=0)
+    return total
 
 
 def shards(target, panel_a, inv_factor, panel_rhs, panel_rows, right_sides):
@@ -31,7 +37,7 @@
         all_tiles = lax.all_gather(column_tiles, "col", axis=0, tiled=True)
         columns = lax.dynamic_slice_in_dim(factor, col_index * shard_rows, shard_rows, 1)
         local_term = jnp.dot(columns, panel_rhs[which_panel], preferred_element_type=jnp.float32)
-        partial_value = lax.psum(local_term, "col").astype(jnp.bfloat16)
+        partial_value = add_all(local_term, "col").astype(jnp.bfloat16)
         pick_rows = (positions[None, :] == row_places[:, None]).astype(jnp.bfloat16)
         pick_cols = (positions[None, :] == col_places[:, None]).astype(jnp.bfloat16)
         row_set = jnp.einsum(

time: 168 us -> 249 us (1.48); the launches traced: 168 us -> 246 us
  waiting for transfers between devices: 0.06 us -> 138 us
  blocking collectives: 119 us -> 49.2 us
  other arithmetic: 0.01 us -> 7.89 us
    all_gather x0 -> x2, waiting for transfers between devices: none -> 90.4 us  [add_all(): parts = lax.all_gather(x, axis, axis=0, tiled=False)]
    psum x1 -> x0, blocking collectives: 69.4 us -> none  [shards(): partial_value = lax.psum(local_term, 'col').astype(jnp.bfloat16)]
    all_gather x2, waiting for transfers between devices: 0.02 us -> 47.4 us  [shards(): all_tiles = lax.all_gather(column_tiles, 'col', axis=0, tiled=True)]
    reduce_sum x0 -> x2, other arithmetic: none -> 7.88 us  [add_all(): total = parts.sum(axis=0)]
  transfers between devices with their start and end apart: 2 -> 4, of which waited for: 0 -> 4; matrix products, arithmetic and copies ran while one was open for 6% -> 14% of each run, Pallas kernels for 0% -> 0%
where the time goes in v1:
time: 249 us; the launch traced here: 246 us
  waiting for transfers between devices  138 us (55%)
  blocking collectives  49.2 us (20%)
  matrix products  27.5 us (11%)
  between operations  13.9 us (6%)
  local copies, waits for them, and re-layouts  9.55 us (4%)
  other arithmetic  7.89 us (3%)
    all_gather x2, waiting for transfers between devices, add_all(): parts = lax.all_gather(x, axis, axis=0, tiled=False)  90.4 us
    all_gather x2, blocking collectives, shards(): column_tiles = lax.all_gather(solved_piece, 'row', axis=1, tiled=True)  49.2 us
    all_gather x2, waiting for transfers between devices, shards(): all_tiles = lax.all_gather(column_tiles, 'col', axis=0, tiled=True)  47.4 us
    dot_general x2, matrix products, shards(): jnp.einsum('ka,axp->kxp', pick_cols, all_tiles, preferred_element_type=jn...  9.4 us
    reduce_sum x2, other arithmetic, add_all(): total = parts.sum(axis=0)  7.88 us
    unnamed x13, local copies, waits for them, and re-layouts  7.19 us
    dot_general x2, matrix products, shards(): jnp.einsum('ia,axp->ixp', pick_rows, all_tiles, preferred_element_type=jn...  5.71 us
  transfers between devices with their start and end apart: 4, of which 4 were waited for; matrix products, arithmetic and copies ran while one was open for 14% of the time, Pallas kernels for 0%

profile of v1, /device:TPU:0, one launch (start us, length us, event | category | flops | bytes accessed | tf_op | source)
XLA Modules:
  0.0 246.1 jit_solution(5081244638563953708)
XLA Ops:
  7.2 1.1 fusion.73
  8.3 1.3 convolution_convert_fusion
  9.6 24.2 %all_gather.26 = bf16[2,128,512]{2,1,0:T(8,128)(2,1)} all-gather(bf16[2,8,512]{2,1,0:T(8,128)(2,1)S(1)} %convolution_convert_fusion), channel_id=1, replica_groups=mesh['row'=16,'col'=16] {'row'}, dimensions={1}, use_global_device_ids=true | all-gather | bytes 278528 | tf_op jit(solution)/shard_map/all_gather | solution.py:36
  33.9 1.3 convolution_convert_fusion.1
  35.2 25.0 %all_gather.24 = bf16[2,128,512]{2,1,0:T(8,128)(2,1)} all-gather(bf16[2,8,512]{2,1,0:T(8,128)(2,1)S(1)} %convolution_convert_fusion.1), channel_id=1, replica_groups=mesh['row'=16,'col'=16] {'row'}, dimensions={1}, use_global_device_ids=true | all-gather | bytes 278528 | tf_op jit(solution)/shard_map/all_gather | solution.py:36
  60.3 1.3 fusion.72
  61.6 1.1 fusion.34
  62.8 1.1 fusion.36
  63.9 13.0 %all-gather.9.cloned.1.call-done = bf16[32,128,512]{2,1,0:T(8,128)(2,1)} async-done(((bf16[2,128,512]{2,1,0:T(8,128)(2,1)}), bf16[32,128,512]{2,1,0:T(8,128)(2,1)}) %all-gather.9.cloned.1.call-update) | async-done | bytes 4194320 | tf_op jit(solution)/shard_map/all_gather | solution.py:37
  76.9 4.7 %fusion.11 = bf16[8,128,512]{2,0,1:T(8,128)(2,1)S(1)} fusion(bf16[32,128,512]{2,1,0:T(8,128)(2,1)} %all-gather.9.cloned.1.call-done, s32[32]{0:T(128)S(1)} %get-tuple-element.10, s32[8]{0:T(128)S(1)} %fusion.68), kind=kOutput, calls=%fused_computation.13 | convolution fusion | flops 34078976 | bytes 5243040 | tf_op jit(solution)/shard_map/ka,axp->kxp/dot_general | solution.py:46
  81.6 3.3 %fusion = bf16[8,128,512]{2,0,1:T(8,128)(2,1)} fusion(bf16[32,128,512]{2,1,0:T(8,128)(2,1)S(1)} %copy-done, s32[32]{0:T(128)S(1)} %get-tuple-element.10, s32[8]{0:T(128)S(1)} %fusion.69), kind=kOutput, calls=%fused_computation.2 | convolution fusion | flops 33554688 | bytes 5243040 | tf_op jit(solution)/shard_map/ia,axp->ixp/dot_general | solution.py:43
  85.0 34.4 %all-gather.7.cloned.1.call-done = bf16[32,128,512]{2,1,0:T(8,128)(2,1)} async-done(((bf16[2,128,512]{2,1,0:T(8,128)(2,1)}), bf16[32,128,512]{2,1,0:T(8,128)(2,1)}) %all-gather.7.cloned.1.call-update) | async-done | bytes 4194320 | tf_op jit(solution)/shard_map/all_gather | solution.py:37
  119.4 4.7 %fusion.8 = bf16[8,128,512]{2,0,1:T(8,128)(2,1)S(1)} fusion(bf16[32,128,512]{2,1,0:T(8,128)(2,1)} %all-gather.7.cloned.1.call-done, s32[32]{0:T(128)S(1)} %get-tuple-element.11, s32[8]{0:T(128)S(1)} %fusion.68), kind=kOutput, calls=%fused_computation.12 | convolution fusion | flops 34078976 | bytes 5243040 | tf_op jit(solution)/shard_map/ka,axp->kxp/dot_general | solution.py:46
  124.1 2.4 fusion.4
  126.5 1.7 fusion.18
  128.2 0.8 copy-done.3
  129.0 2.3 bitcast_subtract_fusion
  131.3 6.3 %copy.26 = f32[8,1,128,8,1,128]{5,4,3,2,1,0:T(1,128)} copy(f32[8,1,128,8,1,128]{5,2,3,0,4,1:T(8,128)S(1)} %bitcast_subtract_fusion) | data formatting | bytes 8388608
  137.6 38.1 %all-gather.13.cloned.1.call-done = f32[8192,256]{1,0:T(8,128)} async-done(((f32[512,256]{1,0:T(8,128)}), f32[8192,256]{1,0:T(8,128)}) %all-gather.13.cloned.1.call-update) | async-done | bytes 8388624 | tf_op jit(solution)/shard_map/all_gather | solution.py:8
  175.7 3.9 %reduce_sum.19 = bf16[512,256]{1,0:T(8,128)(2,1)S(1)} reduce(f32[16,512,256]{2,1,0:T(8,128)} %bitcast.86, f32[]{:T(128)} %constant.24.clone.1), dimensions={0}, to_apply=%region_1.0 | reduce | flops 1966080 | bytes 8650756 | tf_op jit(solution)/shard_map/reduce_sum | solution.py:9
  179.7 52.2 %all-gather.11.cloned.1.call-done = f32[8192,256]{1,0:T(8,128)} async-done(((f32[512,256]{1,0:T(8,128)}), f32[8192,256]{1,0:T(8,128)}) %all-gather.11.cloned.1.call-update) | async-done | bytes 8388624 | tf_op jit(solution)/shard_map/all_gather | solution.py:8
  231.9 3.9 %reduce_sum.18 = bf16[512,256]{1,0:T(8,128)(2,1)S(1)} reduce(f32[16,512,256]{2,1,0:T(8,128)} %bitcast.87, f32[]{:T(128)} %constant.24.clone.1), dimensions={0}, to_apply=%region_0.0 | reduce | flops 1966080 | bytes 8650756 | tf_op jit(solution)/shard_map/reduce_sum | solution.py:9
  235.9 0.7 convolution_bitcast_fusion
  236.6 2.9 %fusion.16 = f32[8,1,128,256]{3,2,1,0:T(8,128)} fusion(f32[8,1,128,256]{3,2,0,1:T(8,128)S(1)} %convolution_bitcast_fusion, f32[8,1,128,256]{3,2,1,0:T(8,128)} %param.11, bf16[8,128,512]{2,0,1:T(8,128)(2,1)S(1)} %fusion.8, bf16[512,256]{1,0:T(8,128)(2,1)S(1)} %reduce_sum.18), kind=kOutput, calls=%fused_computation.18 | convolution fusion | flops 268959744 | bytes 4456448 | tf_op jit(solution)/shard_map/kxp,pn->kxn/dot_general | solution.py:53
  (22 shorter events, 0.3 us)
Async XLA Ops:
  7.2 54.4 %copy-start.4 = (bf16[2,32,256]{2,1,0:T(8,128)(2,1)S(1)}, bf16[2,32,256]{2,1,0:T(8,128)(2,1)}, u32[]{:S(2)}) copy-start(bf16[2,32,256]{2,1,0:T(8,128)(2,1)} %param.9) | copy-start | bytes 98308
  7.2 56.7 %copy-start.5 = (s32[2,32]{1,0:T(2,128)S(1)}, s32[2,32]{1,0:T(2,128)}, u32[]{:S(2)}) copy-start(s32[2,32]{1,0:T(2,128)} %param.10) | copy-start | bytes 772
  7.2 69.7 %all-gather.9.cloned.1.call-start = ((), (), s32[]{:S(2)}) async-start(), calls=%async_computation.1 | async-start | bytes 4456448 | tf_op jit(solution)/shard_map/all_gather | solution.py:37
  33.8 85.6 %all-gather.7.cloned.1.call-start = ((), (), s32[]{:S(2)}) async-start(), calls=%async_computation | async-start | bytes 4456448 | tf_op jit(solution)/shard_map/all_gather | solution.py:37
  60.2 115.5 %all-gather.13.cloned.1.call-start = ((), (), s32[]{:S(2)}) async-start(), calls=%async_computation.3 | async-start | bytes 8912896 | tf_op jit(solution)/shard_map/all_gather | solution.py:8
  62.7 169.2 %all-gather.11.cloned.1.call-start = ((), (), s32[]{:S(2)}) async-start(), calls=%async_computation.2 | async-start | bytes 8912896 | tf_op jit(solution)/shard_map/all_gather | solution.py:8
  76.9 4.7 %copy-start = (bf16[32,128,512]{2,1,0:T(8,128)(2,1)S(1)}, bf16[32,128,512]{2,1,0:T(8,128)(2,1)}, u32[]{:S(2)}) copy-start(bf16[32,128,512]{2,1,0:T(8,128)(2,1)} %all-gather.9.cloned.1.call-done) | copy-start | bytes 12582916
  119.4 4.7 %copy-start.1 = (bf16[32,128,512]{2,1,0:T(8,128)(2,1)S(1)}, bf16[32,128,512]{2,1,0:T(8,128)(2,1)}, u32[]{:S(2)}) copy-start(bf16[32,128,512]{2,1,0:T(8,128)(2,1)} %all-gather.7.cloned.1.call-done) | copy-start | bytes 12582916
  126.5 1.7 copy-start.2
  126.5 2.5 %copy-start.3 = (f32[8,1,128,8,1,128]{5,4,3,2,1,0:T(1,128)S(1)}, f32[8,1,128,8,1,128]{5,4,3,2,1,0:T(1,128)}, u32[]{:S(2)}) copy-start(f32[8,1,128,8,1,128]{5,4,3,2,1,0:T(1,128)} %param.6) | copy-start | bytes 12582916
Sparse Core Ops, SparseCore 0:
  33.9 42.9 all-gather.8
  78.7 40.5 all-gather.6
  121.2 54.4 all-gather.12
  177.4 54.4 all-gather.10
